TPU v7x, 128 devices: a whole 4x4x4 slice. The times are simulated.
128 devices in a mesh: head: 4 (over y), req: 32 (over x, z, core).
Axes of the slice: x: 4, y: 4, z: 4, core: 2. Of those that a mesh axis runs over, the one named last changes fastest.
Arguments:
- hidden_in: bfloat16 [512, 2048], P('req'), may hold values from -40 to 40
- gain_attn: float32 [2048], replicated, may hold values from 0.1 to 1.9
- gain_moe: float32 [2048], replicated, may hold values from 0.1 to 1.9
- w_query: bfloat16 [2048, 2048], P(None, 'head'), may hold values from -0.125 to 0.125
- w_key: bfloat16 [2048, 2048], P(None, 'head'), may hold values from -0.125 to 0.125
- w_value: bfloat16 [2048, 2048], P(None, 'head'), may hold values from -0.125 to 0.125
- w_out: bfloat16 [2048, 2048], P('head'), may hold values from -0.47851562 to 0.47851562
- w_router: bfloat16 [2048, 64], replicated, may hold values from -32 to 32
- w_gate: bfloat16 [64, 2048, 1024], P('req', None, 'head'), may hold values from -0.125 to 0.125
- w_up: bfloat16 [64, 2048, 1024], P('req', None, 'head'), may hold values from -0.125 to 0.125
- w_down: bfloat16 [64, 1024, 2048], P('req', 'head'), may hold values from -1.5 to 1.5
- cache_kv: bfloat16 [2, 256, 256, 2048], P(None, 'req', None, 'head'), may hold values from -210 to 210
- parked_kv: bfloat16 [2, 256, 256, 2048], P(None, 'req', None, 'head'), may hold values from -210 to 210
- lengths: int32 [512], replicated, may hold values from 1 to 256, 65536 in all
- cache_source: int32 [256], replicated, may hold values from 0 to 255, each once
- expert_ids: int32 [512, 8], P('req'), may hold values from 0 to 63, all different within a row; in each aligned block of 16 rows (0 to 15, 16 to 31, ...) at most 4 rows name the same one
Outputs:
- layer_out: bfloat16 [512, 2048], P('req', 'head')
Inputs may be any that keep to these rules, and one draw needn't show every extreme that they name: `cache_source`: every parked row belongs to exactly one continuing request. `expert_ids`: in each aligned block of 16 rows no expert is named by more than 4 rows, a bound that some block reaches.
All inputs are finite; a program needn't handle non-finite values.
Results may differ from a plain program's by a relative error of at most 0.025.
Values may be sent and summed in bfloat16 or wider, within the bound.
A program may use at most 128 MiB of HBM per device.

v0:
```python
import jax
import jax.numpy as jnp
from jax import lax
from jax.sharding import PartitionSpec as P

D = 2048
H = 16
E = 64
epsilon = 1e-06
rope_base = 50000.0


def rms_scale(inputs, gain):
    inputs = inputs.astype(jnp.float32)
    inverse = lax.rsqrt(jnp.mean(inputs * inputs, axis=-1, keepdims=True) + epsilon)
    return inputs * inverse * gain


def rotate(vectors, positions):
    half_dim = vectors.shape[-1] // 2
    frequency = rope_base ** (-2.0 * jnp.arange(half_dim, dtype=jnp.float32) / vectors.shape[-1])
    angles = positions.astype(jnp.float32)[:, None] * frequency[None, :]
    cosine = jnp.cos(angles)[:, None, :]
    sine_part = jnp.sin(angles)[:, None, :]
    leading = vectors[..., :half_dim]
    trailing = vectors[..., half_dim:]
    return jnp.concatenate(
        [leading * cosine - trailing * sine_part, trailing * cosine + leading * sine_part], axis=-1
    )


def cache_block(queries, cache_rows, row_lengths):
    item_count, span_len = (cache_rows.shape[1], cache_rows.shape[2])
    heads_here, head_dim = (queries.shape[1], queries.shape[2])
    key_rows = cache_rows[0].reshape(item_count, span_len, heads_here, head_dim)
    value_rows = cache_rows[1].reshape(item_count, span_len, heads_here, head_dim)
    scores = jnp.einsum(
        "nhd,njhd->nhj", queries, key_rows, preferred_element_type=jnp.float32
    ) * head_dim ** (-0.5)
    usable = (jnp.arange(span_len, dtype=jnp.int32)[None, :] < row_lengths[:, None])[:, None, :]
    scores = jnp.where(usable, scores, -1e30)
    row_max = jnp.max(scores, axis=-1)
    weights = jnp.where(usable, jnp.exp(scores - row_max[:, :, None]), 0.0)
    row_total = jnp.sum(weights, axis=-1)
    weighted = jnp.einsum(
        "nhj,njhd->nhd",
        weights.astype(jnp.bfloat16),
        value_rows,
        preferred_element_type=jnp.float32,
    )
    return (weighted, row_max, row_total)


def finish(weighted, row_max, row_total, queries, key_new, value_new):
    new_score = jnp.sum(
        queries.astype(jnp.float32) * key_new.astype(jnp.float32), axis=-1
    ) * queries.shape[-1] ** (-0.5)
    joint_max = jnp.maximum(row_max, new_score)
    old_part = jnp.exp(row_max - joint_max)
    new_part = jnp.exp(new_score - joint_max)
    numerator = weighted * old_part[..., None] + new_part[..., None] * value_new.astype(jnp.float32)
    return numerator / (row_total * old_part + new_part)[..., None]


def slot_table(route_ids, expert_total, capacity):
    item_count, picks_per = route_ids.shape
    flat_hot = (
        route_ids.reshape(-1)[:, None] == jnp.arange(expert_total, dtype=jnp.int32)[None, :]
    ).astype(jnp.int32)
    earlier = jnp.cumsum(flat_hot, axis=0) - flat_hot
    slot_rank = jnp.sum(earlier * flat_hot, axis=1)
    slot_hot = (slot_rank[:, None] == jnp.arange(capacity, dtype=jnp.int32)[None, :]).astype(
        jnp.float32
    )
    placed = jnp.einsum("pe,pc->ecp", flat_hot.astype(jnp.float32), slot_hot)
    return placed.reshape(expert_total, capacity, item_count, picks_per).sum(axis=-1)


def body(
    hidden_in,
    gain_attn,
    gain_moe,
    w_query,
    w_key,
    w_value,
    w_out,
    w_router,
    w_gate,
    w_up,
    w_down,
    cache_kv,
    parked_kv,
    lengths,
    cache_source,
    expert_ids,
):
    row_count = hidden_in.shape[0]
    resident = cache_kv.shape[1]
    local_width = w_query.shape[1]
    head_dim = D // H
    local_heads = local_width // head_dim
    req_count = lax.axis_size("req")
    req_index = lax.axis_index("req")
    head_index = lax.axis_index("head")
    highest = lax.Precision.HIGHEST
    normed_attn = rms_scale(hidden_in, gain_attn).astype(jnp.bfloat16)
    own_lengths = lax.dynamic_slice_in_dim(lengths, req_index * row_count, row_count)
    queries = jnp.dot(normed_attn, w_query, preferred_element_type=jnp.float32).reshape(
        row_count, local_heads, head_dim
    )
    queries = rotate(queries, own_lengths).astype(jnp.bfloat16)
    key_new = jnp.dot(normed_attn, w_key, preferred_element_type=jnp.float32).reshape(
        row_count, local_heads, head_dim
    )
    key_new = rotate(key_new, own_lengths).astype(jnp.bfloat16)
    value_new = (
        jnp.dot(normed_attn, w_value, preferred_element_type=jnp.float32)
        .astype(jnp.bfloat16)
        .reshape(row_count, local_heads, head_dim)
    )
    home_weighted, home_max, home_total = cache_block(
        queries[:resident], cache_kv, own_lengths[:resident]
    )
    moving = queries[resident:].reshape(resident, local_width)
    all_moving = lax.all_gather(moving, "req", axis=0, tiled=True)
    slot_ids = req_index * resident + jnp.arange(resident, dtype=jnp.int32)
    owner_hot = cache_source[None, :] == slot_ids[:, None]
    parked_queries = jnp.dot(
        owner_hot.astype(jnp.bfloat16), all_moving, preferred_element_type=jnp.float32
    )
    parked_queries = parked_queries.astype(jnp.bfloat16).reshape(resident, local_heads, head_dim)
    moving_lengths = lengths.reshape(req_count, row_count)[:, resident:].reshape(-1)
    parked_lengths = jnp.sum(jnp.where(owner_hot, moving_lengths[None, :], 0), axis=1)
    park_weighted, park_max, park_total = cache_block(parked_queries, parked_kv, parked_lengths)
    spread = owner_hot.astype(jnp.float32).T
    sent_weighted = jnp.dot(spread, park_weighted.reshape(resident, local_width), precision=highest)
    sent_max = jnp.dot(spread, park_max, precision=highest)
    sent_total = jnp.dot(spread, park_total, precision=highest)
    back_weighted, back_max, back_total = (
        lax.psum_scatter(
            sent_weighted.astype(jnp.bfloat16), "req", scatter_dimension=0, tiled=True
        ).astype(jnp.float32),
        lax.psum_scatter(
            sent_max.astype(jnp.bfloat16), "req", scatter_dimension=0, tiled=True
        ).astype(jnp.float32),
        lax.psum_scatter(
            sent_total.astype(jnp.bfloat16), "req", scatter_dimension=0, tiled=True
        ).astype(jnp.float32),
    )
    weighted = jnp.concatenate(
        [home_weighted, back_weighted.reshape(resident, local_heads, head_dim)], axis=0
    )
    row_max = jnp.concatenate([home_max, back_max], axis=0)
    row_total = jnp.concatenate([home_total, back_total], axis=0)
    attended = (
        finish(weighted, row_max, row_total, queries, key_new, value_new)
        .astype(jnp.bfloat16)
        .reshape(row_count, local_width)
    )
    head_terms = jnp.dot(attended, w_out, preferred_element_type=jnp.float32)
    residual = hidden_in.astype(jnp.float32) + lax.psum(
        head_terms.astype(jnp.bfloat16), "head"
    ).astype(jnp.float32)
    normed_moe = rms_scale(residual, gain_moe).astype(jnp.bfloat16)
    logits = jnp.dot(normed_moe, w_router, preferred_element_type=jnp.float32)
    expert_hot = expert_ids[:, :, None] == jnp.arange(E, dtype=jnp.int32)[None, None, :]
    chosen_logits = jnp.sum(jnp.where(expert_hot, logits[:, None, :], 0.0), axis=-1)
    gate_values = jax.nn.softmax(chosen_logits, axis=-1)
    gate_table = jnp.sum(jnp.where(expert_hot, gate_values[:, :, None], 0.0), axis=1)
    capacity = row_count // 4
    slot_map = slot_table(expert_ids, E, capacity)
    mix_weights = slot_map * gate_table.T[:, None, :]
    local_experts = w_gate.shape[0]
    outgoing = jnp.einsum(
        "ecn,nd->ecd", slot_map.astype(jnp.bfloat16), normed_moe, preferred_element_type=jnp.float32
    ).astype(jnp.bfloat16)
    outgoing = outgoing.reshape(req_count, local_experts, capacity, -1)
    arrived = lax.all_to_all(outgoing, "req", split_axis=0, concat_axis=0, tiled=True)
    gate_part = jnp.einsum("secd,edf->secf", arrived, w_gate, preferred_element_type=jnp.float32)
    up_part = jnp.einsum("secd,edf->secf", arrived, w_up, preferred_element_type=jnp.float32)
    hidden = (jax.nn.silu(gate_part) * up_part).astype(jnp.bfloat16)
    partial_out = jnp.einsum("secf,efd->secd", hidden, w_down, preferred_element_type=jnp.float32)
    result = lax.all_to_all(
        partial_out.astype(jnp.bfloat16), "req", split_axis=0, concat_axis=0, tiled=True
    ).astype(partial_out.dtype)
    returned = result
    returned = returned.reshape(E, capacity, -1)
    mixture = jnp.einsum("ecn,ecd->nd", mix_weights, returned, precision=highest)
    share = lax.psum_scatter(
        mixture.astype(jnp.bfloat16), "head", scatter_dimension=1, tiled=True
    ).astype(jnp.float32)
    own_residual = lax.dynamic_slice_in_dim(
        residual, head_index * share.shape[1], share.shape[1], axis=1
    )
    return (own_residual + share).astype(jnp.bfloat16)


def solution(mesh):
    placed = (
        P("req", None),
        P(),
        P(),
        P(None, "head"),
        P(None, "head"),
        P(None, "head"),
        P("head", None),
        P(),
        P("req", None, "head"),
        P("req", None, "head"),
        P("req", "head", None),
        P(None, "req", None, "head"),
        P(None, "req", None, "head"),
        P(),
        P(),
        P("req", None),
    )
    return jax.shard_map(
        body, mesh=mesh, in_specs=placed, out_specs=P("req", "head"), check_vma=False
    )
```

profile of v0, /device:TPU:0, one launch (start us, length us, event | category | flops | bytes accessed | tf_op | source)
XLA Modules:
  0.0 269.1 jit_solution(12115318070932877573)
XLA Ops:
  6.6 1.1 fusion.40
  7.7 0.8 reshape.263
  8.5 0.8 fusion.110
  9.4 0.9 fusion.84
  10.3 2.1 fusion.104
  12.5 2.0 fusion.106
  14.8 26.2 %all_gather.3 = bf16[256,512]{1,0:T(8,128)(2,1)S(1)} all-gather(bf16[8,512]{1,0:T(8,128)(2,1)S(1)} %bitcast.150), channel_id=1, replica_groups=mesh['head'=4,'req'=32] {'req'}, dimensions={0}, use_global_device_ids=true | all-gather | bytes 270336 | tf_op jit(solution)/shard_map/all_gather | solution.py:125
  41.0 0.2 fusion.30
  41.2 4.6 %fusion.112 = (bf16[1,8,256,512]{3,2,1,0:T(8,128)(2,1)}, bf16[1,8,256,512]{3,2,1,0:T(8,128)(2,1)}) fusion(bf16[2,8,256,512]{3,2,1,0:T(8,128)(2,1)} %param.28), kind=kLoop, calls=%fused_computation.149 | loop fusion | bytes 8388608 | tf_op jit(solution)/shard_map/slice | solution.py:36
  45.8 4.0 %reshape_squeeze.15 = bf16[8,256,4,128]{3,2,1,0:T(4,128)(2,1)} reshape(bf16[1,8,256,512]{3,2,1,0:T(8,128)(2,1)} %get-tuple-element.14) | data formatting | bytes 4194304 | tf_op jit(solution)/shard_map/reshape;squeeze | solution.py:36
  49.8 3.9 %copy.94 = bf16[1,8,256,512]{2,3,1,0:T(8,128)(2,1)} copy(bf16[1,8,256,512]{3,2,1,0:T(8,128)(2,1)} %get-tuple-element.15) | data formatting | bytes 4194304 | tf_op jit(solution)/shard_map/reshape;squeeze | solution.py:35
  53.7 2.1 fusion.74
  55.9 0.2 fusion.70
  56.1 0.4 fusion.7
  56.5 1.2 convolution_convert_fusion.3
  57.8 0.2 convolution_convert_fusion.7
  58.2 0.2 multiply_reduce_fusion.1
  58.6 4.6 %fusion.111 = (bf16[1,8,256,512]{3,2,1,0:T(8,128)(2,1)}, bf16[1,8,256,512]{3,2,1,0:T(8,128)(2,1)}) fusion(bf16[2,8,256,512]{3,2,1,0:T(8,128)(2,1)} %param.27), kind=kLoop, calls=%fused_computation.148 | loop fusion | bytes 8388608 | tf_op jit(solution)/shard_map/slice | solution.py:36
  63.1 4.0 %reshape_squeeze.13 = bf16[8,256,4,128]{3,2,1,0:T(4,128)(2,1)} reshape(bf16[1,8,256,512]{3,2,1,0:T(8,128)(2,1)} %get-tuple-element.12) | data formatting | bytes 4194304 | tf_op jit(solution)/shard_map/reshape;squeeze | solution.py:36
  67.1 3.9 %copy.93 = bf16[1,8,256,512]{2,3,1,0:T(8,128)(2,1)} copy(bf16[1,8,256,512]{3,2,1,0:T(8,128)(2,1)} %get-tuple-element.13) | data formatting | bytes 4194304 | tf_op jit(solution)/shard_map/reshape;squeeze | solution.py:35
  71.0 2.0 fusion.76
  73.1 0.2 fusion.71
  73.3 0.2 convolution_convert_fusion.6
  73.5 0.6 dynamic-slice
  74.8 2.0 fusion.9
  76.7 65.3 %all-reduce.2 = (bf16[256,4]{0,1:T(4,128)(2,1)S(1)}, bf16[256,4]{0,1:T(4,128)(2,1)S(1)}) all-reduce(bf16[256,4]{0,1:T(4,128)(2,1)S(1)} %convolution_convert_fusion.7, bf16[256,4]{0,1:T(4,128)(2,1)S(1)} %convolution_convert_fusion.6), channel_id=3, replica_groups=mesh['head'=4,'req'=32] {'req'}, use_global_device_ids=true, to_apply=%region_5.6.clone | all-reduce | flops 2048 | bytes 8192
  142.2 0.2 reduce_window_sum.11
  142.7 0.2 select_reduce_fusion.2
  142.9 0.7 convert_element_type.107
  143.8 3.6 %convolution_convert_fusion.2 = bf16[16,2048]{1,0:T(8,128)(2,1)} fusion(bf16[512,2048]{1,0:T(8,128)(2,1)} %param.22, bf16[2048,512]{1,0:T(8,128)(2,1)} %param.21, f32[2,8,4,128]{3,2,1,0:T(4,128)S(1)} %bitcast.147, f32[2,8,4,128]{3,2,1,0:T(4,128)S(1)} %bitcast.145, f32[2,8,4,128]{3,2,1,0:T(4,128)S(1)} %bitcast.146, f32[8,512]{1,0:T(8,128)S(1)} %convert_element_type.107, ...), kind=kOutput, calls=%fused_computation.5 | convolution fusion | flops 67338240 | bytes 4464704 | tf_op jit(solution)/shard_map/dot_general | solution.py:160
  147.5 0.2 bitcast_reduce_fusion
  147.7 37.3 %all-reduce.5.cloned.1.call-done = bf16[16,2048]{1,0:T(8,128)(2,1)} async-done(((bf16[16,2048]{1,0:T(8,128)(2,1)}), bf16[16,2048]{1,0:T(8,128)(2,1)}) %all-reduce.5.cloned.1.call-update) | async-done | bytes 65552 | tf_op jit(solution)/shard_map/psum | solution.py:161
  184.9 1.6 convert_add_fusion
  186.6 1.3 convolution_convert_fusion.1
  187.9 0.8 copy.95
  188.7 23.8 %all_to_all.10 = bf16[32,2,4,2048]{3,2,1,0:T(4,128)(2,1)S(1)} all-to-all(bf16[32,2,4,2048]{3,2,1,0:T(4,128)(2,1)S(1)} %bitcast.144), channel_id=1, replica_groups=mesh['head'=4,'req'=32] {'req'}, dimensions={0} | all-to-all | bytes 2097152 | tf_op jit(solution)/shard_map/all_to_all | solution.py:178
  212.6 0.9 fusion.11
  213.5 3.9 %fusion = bf16[32,2,4,2048]{3,0,2,1:T(8,128)(2,1)} fusion(bf16[2,256,2048]{2,1,0:T(8,128)(2,1)S(1)} %copy-done, bf16[2,2048,256]{2,1,0:T(8,128)(2,1)} %param.25, bf16[32,2,4,2048]{3,2,1,0:T(4,128)(2,1)S(1)} %all_to_all.10, f32[32,2,4,256]{3,0,2,1:T(8,128)S(1)} %fusion.11), kind=kOutput, calls=%fused_computation.2 | convolution fusion | flops 537788416 | bytes 6553600 | tf_op jit(solution)/shard_map/secf,efd->secd/dot_general | solution.py:182
  217.4 3.1 %copy.76 = bf16[32,2,4,2048]{3,2,1,0:T(4,128)(2,1)} copy(bf16[32,2,4,2048]{3,0,2,1:T(8,128)(2,1)} %fusion) | data formatting | bytes 2097152 | tf_op jit(solution)/shard_map/convert_element_type | solution.py:184
  220.4 4.1 %all-to-all-start.1 = ((bf16[32,2,4,2048]{3,2,1,0:T(4,128)(2,1)}), bf16[32,2,4,2048]{3,2,1,0:T(4,128)(2,1)S(1)}, u32[]{:S(2)}, u32[]{:S(2)}) async-start(bf16[32,2,4,2048]{3,2,1,0:T(4,128)(2,1)} %copy.76), calls=%async_computation.2 | async-start | bytes 2097152 | tf_op jit(solution)/shard_map/all_to_all | solution.py:183
  224.6 1.2 fusion.101
  225.7 0.2 select_reduce_fusion.1
  226.0 0.2 fusion.86
  226.3 0.1 select_reduce_fusion
  226.4 14.9 %all-to-all-done.1 = bf16[32,2,4,2048]{3,2,1,0:T(4,128)(2,1)S(1)} async-done(((bf16[32,2,4,2048]{3,2,1,0:T(4,128)(2,1)}), bf16[32,2,4,2048]{3,2,1,0:T(4,128)(2,1)S(1)}, u32[]{:S(2)}, u32[]{:S(2)}) %all-to-all-start.1) | async-done | bytes 1048608 | tf_op jit(solution)/shard_map/all_to_all | solution.py:183
  241.3 2.2 fusion.1
  243.5 17.7 %reduce-scatter.7.cloned.1.call-done = bf16[16,512]{1,0:T(8,128)(2,1)} async-done(((bf16[16,2048]{1,0:T(8,128)(2,1)}), bf16[16,512]{1,0:T(8,128)(2,1)}) %reduce-scatter.7.cloned.1.call-update) | async-done | bytes 16400 | tf_op jit(solution)/shard_map/reduce_scatter | solution.py:189
  261.2 1.4 add_convert_fusion
  (59 shorter events, 2.3 us)
Async XLA Ops:
  6.5 206.9 %copy-start = (bf16[2,256,2048]{2,1,0:T(8,128)(2,1)S(1)}, bf16[2,256,2048]{2,1,0:T(8,128)(2,1)}, u32[]{:S(2)}) copy-start(bf16[2,256,2048]{2,1,0:T(8,128)(2,1)} %param.26) | copy-start | bytes 6291460
  6.5 5.9 %copy-start.1 = (bf16[16,2048]{1,0:T(8,128)(2,1)S(1)}, bf16[16,2048]{1,0:T(8,128)(2,1)}, u32[]{:S(2)}) copy-start(bf16[16,2048]{1,0:T(8,128)(2,1)} %param.16) | copy-start | bytes 196612
  6.5 5.9 %copy-start.5 = (f32[2048]{0:T(1024)S(1)}, f32[2048]{0:T(1024)}, u32[]{:S(2)}) copy-start(f32[2048]{0:T(1024)} %param.17) | copy-start | bytes 24580
  6.5 136.3 %reduce-scatter.5.cloned.1.call-start = ((), (), s32[]{:S(2)}) async-start(), calls=%async_computation.4 | async-start | bytes 270336 | tf_op jit(solution)/shard_map/reduce_scatter | solution.py:140
  10.3 30.7 %copy-start.7 = (s32[256]{0:T(256)S(1)}, s32[256]{0:T(256)}, u32[]{:S(2)}) copy-start(s32[256]{0:T(256)} %param.30) | copy-start | bytes 3076
  53.7 2.4 copy-start.2
  53.7 4.3 %copy-start.8 = (s32[16,8]{0,1:T(8,128)S(1)}, s32[16,8]{0,1:T(8,128)}, u32[]{:S(2)}) copy-start(s32[16,8]{0,1:T(8,128)} %param.31) | copy-start | bytes 1540
  57.7 127.2 %all-reduce.5.cloned.1.call-start = ((), (), s32[]{:S(2)}) async-start(), calls=%async_computation.5 | async-start | bytes 131072 | tf_op jit(solution)/shard_map/psum | solution.py:161
  71.0 2.5 copy-start.9
  143.8 42.7 %copy-start.6 = (f32[2048]{0:T(1024)S(1)}, f32[2048]{0:T(1024)}, u32[]{:S(2)}) copy-start(f32[2048]{0:T(1024)} %param.18) | copy-start | bytes 24580
  187.9 24.7 %copy-start.3 = (bf16[2,2048,256]{2,1,0:T(8,128)(2,1)S(1)}, bf16[2,2048,256]{2,1,0:T(8,128)(2,1)}, u32[]{:S(2)}) copy-start(bf16[2,2048,256]{2,1,0:T(8,128)(2,1)} %param.24) | copy-start | bytes 6291460
  217.4 7.2 %copy-start.4 = (bf16[16,2048]{1,0:T(8,128)(2,1)S(1)}, bf16[16,2048]{1,0:T(8,128)(2,1)}, u32[]{:S(2)}) copy-start(bf16[16,2048]{1,0:T(8,128)(2,1)} %all-reduce.5.cloned.1.call-done) | copy-start | bytes 196612
  220.4 20.9 %all-to-all-start.1 = ((bf16[32,2,4,2048]{3,2,1,0:T(4,128)(2,1)}), bf16[32,2,4,2048]{3,2,1,0:T(4,128)(2,1)S(1)}, u32[]{:S(2)}, u32[]{:S(2)}) async-start(bf16[32,2,4,2048]{3,2,1,0:T(4,128)(2,1)} %copy.76), calls=%async_computation.2 | async-start | bytes 2097152 | tf_op jit(solution)/shard_map/all_to_all | solution.py:183
  224.5 36.7 %reduce-scatter.7.cloned.1.call-start = ((), (), s32[]{:S(2)}) async-start(), calls=%async_computation.6 | async-start | bytes 81920 | tf_op jit(solution)/shard_map/reduce_scatter | solution.py:189
Sparse Core Ops, SparseCore 0:
  57.8 76.4 reduce-scatter.4
  147.6 37.2 all-reduce.4
  243.6 17.5 reduce-scatter.6
where the time goes:
time: 270 us; the launch traced here: 269 us
  blocking collectives  115 us (43%)
  waiting for transfers between devices  69.9 us (26%)
  local copies, waits for them, and re-layouts  31.2 us (12%)
  matrix products  25.4 us (9%)
  between operations  14 us (5%)
  other arithmetic  9.06 us (3%)
  starting transfers between devices  4.14 us (2%)
    unnamed x1, blocking collectives  65.3 us
    psum x1, waiting for transfers between devices, body(): lax.psum(head_terms.astype(jnp.bfloat16), 'head').astype(jnp.float32)  37.3 us
    all_gather x1, blocking collectives, body(): all_moving = lax.all_gather(moving, 'req', axis=0, tiled=True)  26.2 us
    all_to_all x1, blocking collectives, body(): lax.all_to_all(outgoing, 'req', split_axis=0, concat_axis=0, tiled=True)  23.8 us
    reduce_scatter x1, waiting for transfers between devices, body(): lax.psum_scatter(mixture.astype(jnp.bfloat16), 'head', scatter_dimension=...  17.7 us
    all_to_all x1, waiting for transfers between devices, body(): lax.all_to_all(partial_out.astype(jnp.bfloat16), 'req', split_axis=0, con...  14.9 us
    slice x2, local copies, waits for them, and re-layouts, cache_block(): cache_rows[1].reshape(item_count, span_len, heads_here, head_dim)  9.18 us
    another operation x2, local copies, waits for them, and re-layouts, cache_block(): cache_rows[1].reshape(item_count, span_len, heads_here, head_dim)  7.94 us
  transfers between devices with their start and end apart: 4, of which 3 were waited for; matrix products, arithmetic and copies ran while one was open for 8% of the time, Pallas kernels for 0%

commit v1 on v0

--- a/solution.py
+++ b/solution.py
@@ -158,8 +158,8 @@
         .reshape(row_count, local_width)
     )
     head_terms = jnp.dot(attended, w_out, preferred_element_type=jnp.float32)
-    residual = hidden_in.astype(jnp.float32) + lax.psum(
-        head_terms.astype(jnp.bfloat16), "head"
+    residual = hidden_in.astype(jnp.float32) + jnp.sum(
+        lax.all_gather(head_terms.astype(jnp.bfloat16), "head"), axis=0
     ).astype(jnp.float32)
     normed_moe = rms_scale(residual, gain_moe).astype(jnp.bfloat16)
     logits = jnp.dot(normed_moe, w_router, preferred_element_type=jnp.float32)

time: 270 us -> 240 us (0.89)
  waiting for transfers between devices: 69.9 us -> 33 us
  blocking collectives: 115 us -> 124 us
    psum x1 -> x0, waiting for transfers between devices: 37.3 us -> none  [body(): lax.psum(head_terms.astype(jnp.bfloat16), 'head').astype(jnp.float32)]
    all_gather x0 -> x1, blocking collectives: none -> 12.7 us  [body(): lax.all_gather(head_terms.astype(jnp.bfloat16), 'head')]
    all_to_all x1, blocking collectives: 23.8 us -> 19.8 us  [body(): lax.all_to_all(outgoing, 'req', split_axis=0, concat_axis=0, tiled=True)]
  transfers between devices with their start and end apart: 4 -> 3, of which waited for: 3 -> 2; matrix products, arithmetic and copies ran while one was open for 8% -> 9% of each run, Pallas kernels for 0% -> 0%
where the time goes in v1:
time: 240 us; the launch traced here: 239 us
  blocking collectives  124 us (52%)
  waiting for transfers between devices  33 us (14%)
  local copies, waits for them, and re-layouts  31.2 us (13%)
  matrix products  23.9 us (10%)
  between operations  14.3 us (6%)
  other arithmetic  8.27 us (3%)
  starting transfers between devices  4.07 us (2%)
    unnamed x1, blocking collectives  65.4 us
    all_gather x1, blocking collectives, body(): all_moving = lax.all_gather(moving, 'req', axis=0, tiled=True)  26.2 us
    all_to_all x1, blocking collectives, body(): lax.all_to_all(outgoing, 'req', split_axis=0, concat_axis=0, tiled=True)  19.8 us
    reduce_scatter x1, waiting for transfers between devices, body(): lax.psum_scatter(mixture.astype(jnp.bfloat16), 'head', scatter_dimension=...  18 us
    all_to_all x1, waiting for transfers between devices, body(): lax.all_to_all(partial_out.astype(jnp.bfloat16), 'req', split_axis=0, con...  14.9 us
    all_gather x1, blocking collectives, body(): lax.all_gather(head_terms.astype(jnp.bfloat16), 'head')  12.7 us
    slice x2, local copies, waits for them, and re-layouts, cache_block(): cache_rows[1].reshape(item_count, span_len, heads_here, head_dim)  9.18 us
    another operation x2, local copies, waits for them, and re-layouts, cache_block(): cache_rows[1].reshape(item_count, span_len, heads_here, head_dim)  7.94 us
  transfers between devices with their start and end apart: 3, of which 2 were waited for; matrix products, arithmetic and copies ran while one was open for 9% of the time, Pallas kernels for 0%

profile of v1, /device:TPU:0, one launch (start us, length us, event | category | flops | bytes accessed | tf_op | source)
XLA Modules:
  0.0 238.9 jit_solution(920154619747718996)
XLA Ops:
  6.6 1.1 fusion.40
  7.7 0.8 reshape.263
  8.5 0.8 fusion.110
  9.4 0.9 fusion.84
  10.3 2.1 fusion.104
  12.5 2.0 fusion.106
  14.8 26.2 %all_gather.9 = bf16[256,512]{1,0:T(8,128)(2,1)S(1)} all-gather(bf16[8,512]{1,0:T(8,128)(2,1)S(1)} %bitcast.152), channel_id=1, replica_groups=mesh['head'=4,'req'=32] {'req'}, dimensions={0}, use_global_device_ids=true | all-gather | bytes 270336 | tf_op jit(solution)/shard_map/all_gather | solution.py:125
  41.0 0.2 fusion.30
  41.2 4.6 %fusion.112 = (bf16[1,8,256,512]{3,2,1,0:T(8,128)(2,1)}, bf16[1,8,256,512]{3,2,1,0:T(8,128)(2,1)}) fusion(bf16[2,8,256,512]{3,2,1,0:T(8,128)(2,1)} %param.28), kind=kLoop, calls=%fused_computation.149 | loop fusion | bytes 8388608 | tf_op jit(solution)/shard_map/slice | solution.py:36
  45.8 4.0 %reshape_squeeze.15 = bf16[8,256,4,128]{3,2,1,0:T(4,128)(2,1)} reshape(bf16[1,8,256,512]{3,2,1,0:T(8,128)(2,1)} %get-tuple-element.14) | data formatting | bytes 4194304 | tf_op jit(solution)/shard_map/reshape;squeeze | solution.py:36
  49.8 3.9 %copy.94 = bf16[1,8,256,512]{2,3,1,0:T(8,128)(2,1)} copy(bf16[1,8,256,512]{3,2,1,0:T(8,128)(2,1)} %get-tuple-element.15) | data formatting | bytes 4194304 | tf_op jit(solution)/shard_map/reshape;squeeze | solution.py:35
  53.7 2.1 fusion.74
  55.9 0.2 fusion.70
  56.1 0.4 fusion.7
  56.5 1.2 convolution_convert_fusion.3
  57.7 0.2 convolution_convert_fusion.7
  58.2 0.2 multiply_reduce_fusion.1
  58.5 0.2 reduce_window_sum.11
  58.7 4.6 %fusion.111 = (bf16[1,8,256,512]{3,2,1,0:T(8,128)(2,1)}, bf16[1,8,256,512]{3,2,1,0:T(8,128)(2,1)}) fusion(bf16[2,8,256,512]{3,2,1,0:T(8,128)(2,1)} %param.27), kind=kLoop, calls=%fused_computation.148 | loop fusion | bytes 8388608 | tf_op jit(solution)/shard_map/slice | solution.py:36
  63.3 4.0 %reshape_squeeze.13 = bf16[8,256,4,128]{3,2,1,0:T(4,128)(2,1)} reshape(bf16[1,8,256,512]{3,2,1,0:T(8,128)(2,1)} %get-tuple-element.12) | data formatting | bytes 4194304 | tf_op jit(solution)/shard_map/reshape;squeeze | solution.py:36
  67.2 3.9 %copy.93 = bf16[1,8,256,512]{2,3,1,0:T(8,128)(2,1)} copy(bf16[1,8,256,512]{3,2,1,0:T(8,128)(2,1)} %get-tuple-element.13) | data formatting | bytes 4194304 | tf_op jit(solution)/shard_map/reshape;squeeze | solution.py:35
  71.2 2.0 fusion.76
  73.3 0.2 fusion.71
  73.4 0.2 convolution_convert_fusion.6
  73.6 0.6 dynamic-slice
  74.9 2.0 fusion.9
  76.9 65.4 %all-reduce.2 = (bf16[256,4]{0,1:T(4,128)(2,1)S(1)}, bf16[256,4]{0,1:T(4,128)(2,1)S(1)}) all-reduce(bf16[256,4]{0,1:T(4,128)(2,1)S(1)} %convolution_convert_fusion.7, bf16[256,4]{0,1:T(4,128)(2,1)S(1)} %convolution_convert_fusion.6), channel_id=4, replica_groups=mesh['head'=4,'req'=32] {'req'}, use_global_device_ids=true, to_apply=%region_5.6.clone | all-reduce | flops 2048 | bytes 8192
  142.4 0.2 select_reduce_fusion.2
  142.8 0.2 bitcast_reduce_fusion
  143.0 0.7 convert_element_type.109
  144.0 3.0 %convolution_convert_fusion.2 = bf16[16,2048]{1,0:T(8,128)(2,1)S(1)} fusion(bf16[512,2048]{1,0:T(8,128)(2,1)} %param.22, bf16[2048,512]{1,0:T(8,128)(2,1)} %param.21, f32[2,8,4,128]{3,2,1,0:T(4,128)S(1)} %bitcast.149, f32[2,8,4,128]{3,2,1,0:T(4,128)S(1)} %bitcast.147, f32[2,8,4,128]{3,2,1,0:T(4,128)S(1)} %bitcast.148, ...), kind=kOutput, calls=%fused_computation.5 | convolution fusion | flops 67338240 | bytes 4464704 | tf_op jit(solution)/shard_map/dot_general | solution.py:160
  147.0 12.7 %all-gather = bf16[64,2048]{1,0:T(8,128)(2,1)S(1)} all-gather(bf16[16,2048]{1,0:T(8,128)(2,1)S(1)} %convolution_convert_fusion.2), channel_id=2, replica_groups=mesh['head'=4,'req'=32] {'head'}, dimensions={0}, use_global_device_ids=true | all-gather | bytes 327680 | tf_op jit(solution)/shard_map/all_gather | solution.py:162
  159.8 0.8 convert_add_fusion
  160.6 0.5 convolution_convert_fusion.1
  161.1 0.8 copy.95
  161.9 19.8 %all_to_all.10 = bf16[32,2,4,2048]{3,2,1,0:T(4,128)(2,1)S(1)} all-to-all(bf16[32,2,4,2048]{3,2,1,0:T(4,128)(2,1)S(1)} %bitcast.145), channel_id=1, replica_groups=mesh['head'=4,'req'=32] {'req'}, dimensions={0} | all-to-all | bytes 2097152 | tf_op jit(solution)/shard_map/all_to_all | solution.py:178
  181.7 0.9 fusion.11
  182.6 3.9 %fusion = bf16[32,2,4,2048]{3,0,2,1:T(8,128)(2,1)} fusion(bf16[2,256,2048]{2,1,0:T(8,128)(2,1)S(1)} %copy-done, bf16[2,2048,256]{2,1,0:T(8,128)(2,1)} %param.25, bf16[32,2,4,2048]{3,2,1,0:T(4,128)(2,1)S(1)} %all_to_all.10, f32[32,2,4,256]{3,0,2,1:T(8,128)S(1)} %fusion.11), kind=kOutput, calls=%fused_computation.2 | convolution fusion | flops 537788416 | bytes 6553600 | tf_op jit(solution)/shard_map/secf,efd->secd/dot_general | solution.py:182
  186.5 3.1 %copy.76 = bf16[32,2,4,2048]{3,2,1,0:T(4,128)(2,1)} copy(bf16[32,2,4,2048]{3,0,2,1:T(8,128)(2,1)} %fusion) | data formatting | bytes 2097152 | tf_op jit(solution)/shard_map/convert_element_type | solution.py:184
  189.6 4.0 %all-to-all-start.1 = ((bf16[32,2,4,2048]{3,2,1,0:T(4,128)(2,1)}), bf16[32,2,4,2048]{3,2,1,0:T(4,128)(2,1)S(1)}, u32[]{:S(2)}, u32[]{:S(2)}) async-start(bf16[32,2,4,2048]{3,2,1,0:T(4,128)(2,1)} %copy.76), calls=%async_computation.2 | async-start | bytes 2097152 | tf_op jit(solution)/shard_map/all_to_all | solution.py:183
  193.7 1.2 fusion.101
  194.9 0.2 select_reduce_fusion.1
  195.2 0.2 fusion.86
  195.4 0.1 select_reduce_fusion
  195.6 14.9 %all-to-all-done.1 = bf16[32,2,4,2048]{3,2,1,0:T(4,128)(2,1)S(1)} async-done(((bf16[32,2,4,2048]{3,2,1,0:T(4,128)(2,1)}), bf16[32,2,4,2048]{3,2,1,0:T(4,128)(2,1)S(1)}, u32[]{:S(2)}, u32[]{:S(2)}) %all-to-all-start.1) | async-done | bytes 1048608 | tf_op jit(solution)/shard_map/all_to_all | solution.py:183
  210.5 2.2 fusion.1
  212.6 18.0 %reduce-scatter.7.cloned.1.call-done = bf16[16,512]{1,0:T(8,128)(2,1)} async-done(((bf16[16,2048]{1,0:T(8,128)(2,1)}), bf16[16,512]{1,0:T(8,128)(2,1)}) %reduce-scatter.7.cloned.1.call-update) | async-done | bytes 16400 | tf_op jit(solution)/shard_map/reduce_scatter | solution.py:189
  230.7 1.4 add_convert_fusion
  (64 shorter events, 2.3 us)
Async XLA Ops:
  6.5 176.1 %copy-start = (bf16[2,256,2048]{2,1,0:T(8,128)(2,1)S(1)}, bf16[2,256,2048]{2,1,0:T(8,128)(2,1)}, u32[]{:S(2)}) copy-start(bf16[2,256,2048]{2,1,0:T(8,128)(2,1)} %param.26) | copy-start | bytes 6291460
  6.5 5.9 %copy-start.1 = (bf16[16,2048]{1,0:T(8,128)(2,1)S(1)}, bf16[16,2048]{1,0:T(8,128)(2,1)}, u32[]{:S(2)}) copy-start(bf16[16,2048]{1,0:T(8,128)(2,1)} %param.16) | copy-start | bytes 196612
  6.5 5.9 %copy-start.6 = (f32[2048]{0:T(1024)S(1)}, f32[2048]{0:T(1024)}, u32[]{:S(2)}) copy-start(f32[2048]{0:T(1024)} %param.17) | copy-start | bytes 24580
  6.5 136.5 %reduce-scatter.5.cloned.1.call-start = ((), (), s32[]{:S(2)}) async-start(), calls=%async_computation.4 | async-start | bytes 270336 | tf_op jit(solution)/shard_map/reduce_scatter | solution.py:140
  10.3 30.7 %copy-start.8 = (s32[256]{0:T(256)S(1)}, s32[256]{0:T(256)}, u32[]{:S(2)}) copy-start(s32[256]{0:T(256)} %param.30) | copy-start | bytes 3076
  53.7 2.4 %copy-start.2 = (bf16[8,256,4,128]{3,2,1,0:T(4,128)(2,1)S(1)}, bf16[8,256,4,128]{3,2,1,0:T(4,128)(2,1)}, u32[]{:S(2)}) copy-start(bf16[8,256,4,128]{3,2,1,0:T(4,128)(2,1)} %reshape_squeeze.15) | copy-start | bytes 6291460
  53.7 4.3 %copy-start.9 = (s32[16,8]{0,1:T(8,128)S(1)}, s32[16,8]{0,1:T(8,128)}, u32[]{:S(2)}) copy-start(s32[16,8]{0,1:T(8,128)} %param.31) | copy-start | bytes 1540
  71.2 2.5 %copy-start.12 = (u32[128]{0:T(128)S(1)}, u32[128]{0:T(128)}, u32[]{:S(2)}) copy-start(u32[128]{0:T(128)} %constant.60) | copy-start | bytes 1540
  143.0 17.6 %copy-start.4 = (f32[64,4,16]{0,2,1:T(8,128)}, f32[64,4,16]{0,2,1:T(8,128)S(1)}, u32[]{:S(2)}) copy-start(f32[64,4,16]{0,2,1:T(8,128)S(1)} %bitcast_reduce_fusion) | copy-start | bytes 49156
  144.0 16.6 %copy-start.7 = (f32[2048]{0:T(1024)S(1)}, f32[2048]{0:T(1024)}, u32[]{:S(2)}) copy-start(f32[2048]{0:T(1024)} %param.18) | copy-start | bytes 24580
  160.6 1.3 copy-start.10
  161.1 20.6 %copy-start.3 = (bf16[2,2048,256]{2,1,0:T(8,128)(2,1)S(1)}, bf16[2,2048,256]{2,1,0:T(8,128)(2,1)}, u32[]{:S(2)}) copy-start(bf16[2,2048,256]{2,1,0:T(8,128)(2,1)} %param.24) | copy-start | bytes 6291460
  186.5 7.2 %copy-start.11 = (f32[16]{0:T(128)S(1)}, f32[16]{0:T(128)}, u32[]{:S(2)}) copy-start(f32[16]{0:T(128)} %copy-done.10) | copy-start | bytes 196
  186.5 23.9 %copy-start.5 = (f32[64,4,16]{0,2,1:T(8,128)S(1)}, f32[64,4,16]{0,2,1:T(8,128)}, u32[]{:S(2)}) copy-start(f32[64,4,16]{0,2,1:T(8,128)} %copy-done.4) | copy-start | bytes 49156
  189.6 20.8 %all-to-all-start.1 = ((bf16[32,2,4,2048]{3,2,1,0:T(4,128)(2,1)}), bf16[32,2,4,2048]{3,2,1,0:T(4,128)(2,1)S(1)}, u32[]{:S(2)}, u32[]{:S(2)}) async-start(bf16[32,2,4,2048]{3,2,1,0:T(4,128)(2,1)} %copy.76), calls=%async_computation.2 | async-start | bytes 2097152 | tf_op jit(solution)/shard_map/all_to_all | solution.py:183
  193.6 37.0 %reduce-scatter.7.cloned.1.call-start = ((), (), s32[]{:S(2)}) async-start(), calls=%async_computation.5 | async-start | bytes 81920 | tf_op jit(solution)/shard_map/reduce_scatter | solution.py:189
Sparse Core Ops, SparseCore 0:
  57.8 76.4 reduce-scatter.4
  212.8 17.8 reduce-scatter.6
